TPU v7x, 256 devices: a whole 4x4x8 slice. The times are simulated.
256 devices in a mesh: dp: 4 (over x), tensor: 64 (over y, z, core).
Axes of the slice: x: 4, y: 4, z: 8, core: 2. Of those that a mesh axis runs over, the one named last changes fastest.
Arguments:
- grad_out: bfloat16 [4096, 8192], P('dp', 'tensor'), may hold values from -6 to 6
- acts: bfloat16 [4096, 16384], P('dp', 'tensor'), may hold values from -6 to 6
- weight: bfloat16 [8192, 16384], P('tensor'), may hold values from -0.078125 to 0.078125
- block_mask: int32 [64, 128], replicated, may hold values from 0 to 1, as said below
Outputs:
- grad_acts: bfloat16 [4096, 16384], P('dp', 'tensor')
- grad_weight: float32 [8192, 16384], P(('dp', 'tensor'))
Inputs may be any that keep to these rules, and one draw needn't show every extreme that they name: `block_mask`: kept shares differ between groups of 2 consecutive block columns, from about three twentieths to nine twentieths.
All inputs are finite; a program needn't handle non-finite values.
Results may differ from a plain program's by a relative error of at most 0.001.
Values may be sent and summed in bfloat16 or wider, within the bound.
A program may use at most 128 MiB of HBM per device.

v0:
```python
import jax
import jax.numpy as jnp
from jax import lax
from jax.sharding import PartitionSpec as P


def expand_mask(mask, side):
    rows, cols = mask.shape
    full = jnp.broadcast_to(mask[:, None, :, None], (rows, side, cols, side))
    return full.reshape(rows * side, cols * side)


def body(grad_out, acts, weight, block_mask):
    tensor_count = lax.axis_size("tensor")
    group_count = lax.axis_size("dp")
    position = lax.axis_index("tensor")
    d_tile = weight.shape[0]
    full_width = weight.shape[1]
    ff_tile = acts.shape[1]
    side = full_width // block_mask.shape[1]
    total_rows = d_tile * tensor_count
    row_mask = lax.dynamic_slice_in_dim(block_mask, position * (d_tile // side), d_tile // side, 0)
    kept = weight * expand_mask(row_mask, side).astype(jnp.bfloat16)
    columns = lax.all_to_all(kept, "tensor", split_axis=1, concat_axis=0, tiled=True)
    piece = lax.all_gather(grad_out, "tensor", axis=1, tiled=True)
    input_grad = jnp.dot(piece, columns, preferred_element_type=jnp.float32)
    grad_rows = lax.dot_general(
        piece, acts, (((0,), (0,)), ((), ())), preferred_element_type=jnp.float32
    )
    weight_grad = grad_rows
    input_grad, weight_grad = (input_grad, weight_grad)
    grad_acts = input_grad.astype(jnp.bfloat16)
    col_mask = lax.dynamic_slice_in_dim(
        block_mask, position * (ff_tile // side), ff_tile // side, 1
    )
    scale_factor = 1.0 / (grad_out.shape[0] * group_count) ** 0.5
    weight_grad = weight_grad * expand_mask(col_mask, side).astype(jnp.float32) * scale_factor
    quarter = total_rows // (group_count * tensor_count)
    reordered = weight_grad.reshape(group_count, tensor_count, quarter, ff_tile)
    reordered = jnp.transpose(reordered, (1, 0, 2, 3)).reshape(total_rows, ff_tile)
    owned = lax.all_to_all(reordered, "tensor", split_axis=0, concat_axis=1, tiled=True)
    grad_weight = lax.psum_scatter(owned, "dp", scatter_dimension=0, tiled=True)
    return (grad_acts, grad_weight)


def solution(mesh):
    in_specs = (P("dp", "tensor"), P("dp", "tensor"), P("tensor", None), P())
    out_specs = (P("dp", "tensor"), P(("dp", "tensor"), None))
    return jax.shard_map(body, mesh=mesh, in_specs=in_specs, out_specs=out_specs, check_vma=False)
```

profile of v0, /device:TPU:1, one launch (start us, length us, event | category | flops | bytes accessed | tf_op | source)
XLA Modules:
  0.0 497.6 jit_solution(10132291511642374837)
XLA Ops:
  7.2 0.0 copy-start
  7.2 0.0 all-gather.2.cloned.1.call-start
  7.2 0.7 all-gather.2.cloned.1.call-update
  7.9 0.0 reduce-scatter.4.cloned.1.call-start
  8.0 0.8 dynamic-slice_convert_fusion
  8.8 113.1 %all-gather.2.cloned.1.call-done = bf16[1024,8192]{1,0:T(8,128)(2,1)} async-done(((bf16[1024,128]{1,0:T(8,128)(2,1)}), bf16[1024,8192]{1,0:T(8,128)(2,1)}) %all-gather.2.cloned.1.call-update) | async-done | bytes 16777232 | tf_op jit(solution)/shard_map/all_gather | solution.py:25
  121.9 5.5 %broadcast_in_dim.16 = f32[64,128,2,128]{3,2,1,0:T(2,128)} broadcast(f32[64,2]{1,0:T(8,128)S(1)} %dynamic-slice_convert_fusion), dimensions={0,2} | broadcast | bytes 8389120 | tf_op jit(solution)/shard_map/broadcast_in_dim | solution.py:9
  127.4 0.0 copy-done
  127.4 13.7 %fusion = f32[8192,256]{1,0:T(8,128)S(1)} fusion(bf16[1024,8192]{1,0:T(8,128)(2,1)} %all-gather.2.cloned.1.call-done, bf16[1024,256]{1,0:T(8,128)(2,1)S(1)} %copy-done, f32[1024,8,2,128]{3,2,1,0:T(2,128)} %bitcast.29), kind=kOutput, calls=%fused_computation.1 | convolution fusion | flops 4299161600 | bytes 34078720 | tf_op jit(solution)/shard_map/dot_general | solution.py:27
  141.1 1.7 copy.17
  142.7 192.2 %all_to_all.38 = f32[64,128,256]{2,1,0:T(8,128)} all-to-all(f32[64,128,256]{2,1,0:T(8,128)S(1)} %bitcast.24), channel_id=1, replica_groups=mesh['dp'=4,'tensor'=64] {'tensor'}, dimensions={0} | all-to-all | bytes 16777216 | tf_op jit(solution)/shard_map/all_to_all | solution.py:41
  334.9 9.0 %copy.18 = f32[128,64,256]{0,2,1:T(8,128)} copy(f32[128,64,256]{2,0,1:T(8,128)} %bitcast.25) | data formatting | bytes 16777216 | tf_op jit(solution)/shard_map/all_to_all | solution.py:41
  343.9 9.0 %copy.21 = f32[128,16384]{1,0:T(8,128)} copy(f32[128,16384]{0,1:T(8,128)} %bitcast.26) | data formatting | bytes 16777216
  352.8 0.0 reduce-scatter.4.cloned.1.call-update
  352.9 6.4 %copy.15 = bf16[128,16384]{0,1:T(8,128)(2,1)} copy(bf16[128,16384]{1,0:T(8,128)(2,1)} %param.6) | data formatting | bytes 8388608 | tf_op args[2]
  359.2 0.7 convert_bitcast_fusion
  359.9 0.1 broadcast_bitcast_fusion
  360.0 10.0 %broadcast_multiply_fusion = bf16[128,16384]{0,1:T(8,128)(2,1)S(1)} fusion(bf16[128,16384]{0,1:T(8,128)(2,1)} %copy.15, bf16[16384]{0:T(1024)(128)(2,1)S(1)} %broadcast_bitcast_fusion), kind=kLoop, calls=%fused_computation.2 | loop fusion | flops 2097152 | bytes 8421376 | tf_op jit(solution)/shard_map/mul | solution.py:23
  370.0 101.7 %all_to_all.39 = bf16[128,64,256]{0,2,1:T(8,128)(2,1)} all-to-all(bf16[128,64,256]{0,2,1:T(8,128)(2,1)S(1)} %bitcast.27), channel_id=1, replica_groups=mesh['dp'=4,'tensor'=64] {'tensor'}, dimensions={1} | all-to-all | bytes 8388608 | tf_op jit(solution)/shard_map/all_to_all | solution.py:24
  471.7 6.4 %copy.16 = bf16[64,128,256]{2,1,0:T(8,128)(2,1)} copy(bf16[64,128,256]{1,2,0:T(8,128)(2,1)} %bitcast.28) | data formatting | bytes 8388608 | tf_op jit(solution)/shard_map/all_to_all | solution.py:24
  478.1 0.0 copy-start.1
  478.1 11.6 %fusion.1 = bf16[1024,256]{0,1:T(8,128)(2,1)S(1)} fusion(bf16[8192,256]{1,0:T(8,128)(2,1)} %bitcast.31, bf16[1024,8192]{1,0:T(8,128)(2,1)} %all-gather.2.cloned.1.call-done), kind=kOutput, calls=%fused_computation.4 | convolution fusion | flops 4295229440 | bytes 21495808 | tf_op jit(solution)/shard_map/dot_general | solution.py:26
  489.8 1.0 copy.19
  490.8 0.0 copy-done.1
  (1 shorter events, 0.0 us)
Async XLA Ops:
  7.2 120.2 %copy-start = (bf16[1024,256]{1,0:T(8,128)(2,1)S(1)}, bf16[1024,256]{1,0:T(8,128)(2,1)}, u32[]{:S(2)}) copy-start(bf16[1024,256]{1,0:T(8,128)(2,1)} %param.5) | copy-start | bytes 1572868
  7.2 114.8 %all-gather.2.cloned.1.call-start = ((), (), s32[]{:S(2)}) async-start(), calls=%async_computation.3 | async-start | bytes 17039360 | tf_op jit(solution)/shard_map/all_gather | solution.py:25
  7.9 482.8 %reduce-scatter.4.cloned.1.call-start = ((), (), s32[]{:S(2)}) async-start(), calls=%async_computation.4 | async-start | bytes 10485760
  478.1 12.7 %copy-start.1 = (bf16[1024,256]{1,0:T(8,128)(2,1)S(1)}, bf16[1024,256]{1,0:T(8,128)(2,1)}, u32[]{:S(2)}) copy-start(bf16[1024,256]{1,0:T(8,128)(2,1)} %param.5) | copy-start | bytes 1572868
Sparse Core Ops, SparseCore 0:
  10.6 111.3 all-gather.1
  353.0 79.4 reduce-scatter.3
where the time goes:
time: 498 us
  blocking collectives  294 us (59%)
  waiting for transfers between devices  114 us (23%)
  local copies, waits for them, and re-layouts  38.9 us (8%)
  matrix products  25.3 us (5%)
  between operations  14.1 us (3%)
  other arithmetic  11.6 us (2%)
    all_to_all x1, blocking collectives, body(): lax.all_to_all(reordered, 'tensor', split_axis=0, concat_axis=1, tiled=True)  192 us
    all_gather x1, waiting for transfers between devices, body(): piece = lax.all_gather(grad_out, 'tensor', axis=1, tiled=True)  113 us
    all_to_all x1, blocking collectives, body(): lax.all_to_all(kept, 'tensor', split_axis=1, concat_axis=0, tiled=True)  102 us
    unnamed x7, local copies, waits for them, and re-layouts  16.3 us
    dot_general x1, matrix products, body(): lax.dot_general(piece, acts, (((0,), (0,)), ((), ())), preferred_element_...  13.7 us
    dot_general x1, matrix products, body(): input_grad = jnp.dot(piece, columns, preferred_element_type=jnp.float32)  11.6 us
    mul x1, other arithmetic, body(): kept = weight * expand_mask(row_mask, side).astype(jnp.bfloat16)  10 us
  transfers between devices with their start and end apart: 2, of which 1 were waited for; matrix products, arithmetic and copies ran while one was open for 7% of the time, Pallas kernels for 0%

commit v1 on v0

--- a/solution.py
+++ b/solution.py
@@ -2,6 +2,27 @@
 import jax.numpy as jnp
 from jax import lax
 from jax.sharding import PartitionSpec as P
+
+
+def in_order(parts, dim):
+    shape = list(parts.shape[1:])
+    shape[dim] *= parts.shape[0]
+    return jnp.moveaxis(parts, 0, dim).reshape(shape)
+
+
+def doubled(x, axis):
+    devices, here = (lax.axis_size(axis), lax.axis_index(axis))
+    tiles, bit = (x[None], 1)
+    while bit < devices:
+        other = lax.ppermute(tiles, axis, [(i, i ^ bit) for i in range(devices)])
+        low = here & bit == 0
+        tiles = jnp.concatenate([jnp.where(low, tiles, other), jnp.where(low, other, tiles)])
+        bit *= 2
+    return tiles
+
+
+def collect(array, axis, dim):
+    return in_order(doubled(array, axis), dim)
 
 
 def expand_mask(mask, side):
@@ -22,7 +43,7 @@
     row_mask = lax.dynamic_slice_in_dim(block_mask, position * (d_tile // side), d_tile // side, 0)
     kept = weight * expand_mask(row_mask, side).astype(jnp.bfloat16)
     columns = lax.all_to_all(kept, "tensor", split_axis=1, concat_axis=0, tiled=True)
-    piece = lax.all_gather(grad_out, "tensor", axis=1, tiled=True)
+    piece = collect(grad_out, "tensor", 1)
     input_grad = jnp.dot(piece, columns, preferred_element_type=jnp.float32)
     grad_rows = lax.dot_general(
         piece, acts, (((0,), (0,)), ((), ())), preferred_element_type=jnp.float32

time: 498 us -> 879 us (1.77)
  waiting for transfers between devices: 114 us -> 420 us
  local copies, waits for them, and re-layouts: 38.9 us -> 67.3 us
  other arithmetic: 11.6 us -> 39.4 us
  starting transfers between devices: 0.08 us -> 13.7 us
    ppermute x0 -> x6, waiting for transfers between devices: none -> 420 us  [doubled(): other = lax.ppermute(tiles, axis, [(i, i ^ bit) for i in range(devices)])]
    all_gather x1 -> x0, waiting for transfers between devices: 113 us -> none  [body(): piece = lax.all_gather(grad_out, 'tensor', axis=1, tiled=True)]
    transpose x0 -> x1, local copies, waits for them, and re-layouts: none -> 22.4 us  [in_order(): return jnp.moveaxis(parts, 0, dim).reshape(shape)]
    select_n x0 -> x6, other arithmetic: none -> 15.4 us  [doubled(): jnp.where(low, tiles, other)]
    ppermute x0 -> x6, starting transfers between devices: none -> 13.7 us  [doubled(): other = lax.ppermute(tiles, axis, [(i, i ^ bit) for i in range(devices)])]
    concatenate x0 -> x5, other arithmetic: none -> 11.3 us  [doubled(): jnp.concatenate([jnp.where(low, tiles, other), jnp.where(low, other, tile...]
    unnamed x7 -> x18, local copies, waits for them, and re-layouts: 16.3 us -> 22.4 us
  transfers between devices with their start and end apart: 2 -> 7, of which waited for: 1 -> 6; matrix products, arithmetic and copies ran while one was open for 7% -> 3% of each run, Pallas kernels for 0% -> 0%
where the time goes in v1:
time: 879 us; the launch traced here: 878 us
  waiting for transfers between devices  420 us (48%)
  blocking collectives  301 us (34%)
  local copies, waits for them, and re-layouts  67.3 us (8%)
  other arithmetic  39.4 us (4%)
  matrix products  22.1 us (3%)
  between operations  14.2 us (2%)
  starting transfers between devices  13.7 us (2%)
    ppermute x6, waiting for transfers between devices, doubled(): other = lax.ppermute(tiles, axis, [(i, i ^ bit) for i in range(devices)])  420 us
    all_to_all x1, blocking collectives, body(): lax.all_to_all(reordered, 'tensor', split_axis=0, concat_axis=1, tiled=True)  198 us
    all_to_all x1, blocking collectives, body(): lax.all_to_all(kept, 'tensor', split_axis=1, concat_axis=0, tiled=True)  102 us
    transpose x1, local copies, waits for them, and re-layouts, in_order(): return jnp.moveaxis(parts, 0, dim).reshape(shape)  22.4 us
    unnamed x18, local copies, waits for them, and re-layouts  22.4 us
  transfers between devices with their start and end apart: 7, of which 6 were waited for; matrix products, arithmetic and copies ran while one was open for 3% of the time, Pallas kernels for 0%

profile of v1, /device:TPU:1, one launch (start us, length us, event | category | flops | bytes accessed | tf_op | source)
XLA Modules:
  0.0 877.6 jit_solution(2927977418075962872)
XLA Ops:
  7.2 3.3 collective-permute-start
  13.1 13.1 %collective-permute-done.1 = bf16[2,1024,128]{2,1,0:T(8,128)(2,1)S(1)} collective-permute-done((bf16[2,1024,128]{2,1,0:T(8,128)(2,1)S(1)}, bf16[2,1024,128]{2,1,0:T(8,128)(2,1)S(1)}, u32[]{:S(2)}, u32[]{:S(2)}) %collective-permute-start.1) | collective-permute-done | bytes 524320 | tf_op jit(solution)/shard_map/ppermute | solution.py:17
  29.0 46.8 %collective-permute-done.2 = bf16[4,1024,128]{2,1,0:T(8,128)(2,1)S(1)} collective-permute-done((bf16[4,1024,128]{2,1,0:T(8,128)(2,1)}, bf16[4,1024,128]{2,1,0:T(8,128)(2,1)S(1)}, u32[]{:S(2)}, u32[]{:S(2)}) %collective-permute-start.2) | collective-permute-done | bytes 1048608 | tf_op jit(solution)/shard_map/ppermute | solution.py:17
  77.2 4.9 collective-permute-start.3
  82.1 90.9 %collective-permute-done.3 = bf16[8,1024,128]{2,1,0:T(8,128)(2,1)} collective-permute-done((bf16[8,1024,128]{2,1,0:T(8,128)(2,1)S(1)}, bf16[8,1024,128]{2,1,0:T(8,128)(2,1)}, u32[]{:S(2)}, u32[]{:S(2)}) %collective-permute-start.3) | collective-permute-done | bytes 2097184 | tf_op jit(solution)/shard_map/ppermute | solution.py:17
  179.2 89.6 %collective-permute-done.4 = bf16[16,1024,128]{2,1,0:T(8,128)(2,1)} collective-permute-done((bf16[16,1024,128]{2,1,0:T(8,128)(2,1)}, bf16[16,1024,128]{2,1,0:T(8,128)(2,1)}, u32[]{:S(2)}, u32[]{:S(2)}) %collective-permute-start.4) | collective-permute-done | bytes 4194336 | tf_op jit(solution)/shard_map/ppermute | solution.py:17
  268.8 5.4 broadcast_select_fusion.3
  274.3 7.4 pad_maximum_fusion
  281.7 2.7 collective-permute-start.5
  284.4 178.4 %collective-permute-done.5 = bf16[32,1024,128]{2,1,0:T(8,128)(2,1)} collective-permute-done((bf16[32,1024,128]{2,1,0:T(8,128)(2,1)}, bf16[32,1024,128]{2,1,0:T(8,128)(2,1)}, u32[]{:S(2)}, u32[]{:S(2)}) %collective-permute-start.5) | collective-permute-done | bytes 8388640 | tf_op jit(solution)/shard_map/ppermute | solution.py:17
  462.9 6.3 broadcast_select_fusion.1
  469.2 3.2 copy-done.2
  474.9 6.7 maximum_bitcast_fusion
  481.7 22.4 %copy.18 = bf16[1024,64,128]{0,2,1:T(8,128)(2,1)} copy(bf16[1024,64,128]{2,0,1:T(8,128)(2,1)} %maximum_bitcast_fusion) | data formatting | bytes 33554432 | tf_op jit(solution)/shard_map/transpose | solution.py:10
  504.1 5.5 broadcast_in_dim.20
  509.5 13.1 %fusion = f32[8192,256]{1,0:T(8,128)S(1)} fusion(bf16[1024,8192]{0,1:T(8,128)(2,1)} %bitcast.36, bf16[1024,256]{1,0:T(8,128)(2,1)S(1)} %copy-done, f32[1024,8,2,128]{3,2,1,0:T(2,128)} %bitcast.37), kind=kOutput, calls=%fused_computation.2 | convolution fusion | flops 4299161600 | bytes 34078720 | tf_op jit(solution)/shard_map/dot_general | solution.py:48
  524.3 198.5 %all_to_all.35 = f32[64,128,256]{2,1,0:T(8,128)} all-to-all(f32[64,128,256]{2,1,0:T(8,128)S(1)} %bitcast.39), channel_id=1, replica_groups=mesh['dp'=4,'tensor'=64] {'tensor'}, dimensions={0} | all-to-all | bytes 16777216 | tf_op jit(solution)/shard_map/all_to_all | solution.py:62
  722.8 9.0 %copy.20 = f32[128,64,256]{0,2,1:T(8,128)} copy(f32[128,64,256]{2,0,1:T(8,128)} %bitcast.40) | data formatting | bytes 16777216 | tf_op jit(solution)/shard_map/all_to_all | solution.py:62
  731.7 9.0 %copy.22 = f32[128,16384]{1,0:T(8,128)} copy(f32[128,16384]{0,1:T(8,128)} %bitcast.41) | data formatting | bytes 16777216
  740.7 6.4 copy.16
  747.2 5.9 broadcast_multiply_fusion
  753.2 6.4 copy.17
  759.6 102.2 %all_to_all.36 = bf16[128,64,256]{2,0,1:T(8,128)(2,1)S(1)} all-to-all(bf16[128,64,256]{2,0,1:T(8,128)(2,1)} %copy.17), channel_id=1, replica_groups=mesh['dp'=4,'tensor'=64] {'tensor'}, dimensions={1} | all-to-all | bytes 8388608 | tf_op jit(solution)/shard_map/all_to_all | solution.py:45
  861.8 9.0 %fusion.6 = bf16[1024,256]{1,0:T(8,128)(2,1)} fusion(bf16[128,64,256]{2,0,1:T(8,128)(2,1)S(1)} %all_to_all.36, bf16[32,1024,128]{2,1,0:T(8,128)(2,1)} %copy-done.3, bf16[32,1024,128]{2,1,0:T(8,128)(2,1)} %copy-done.2), kind=kOutput, calls=%fused_computation.16 | convolution fusion | flops 4303618048 | bytes 21495808 | tf_op jit(solution)/shard_map/dot_general | solution.py:47
  (34 shorter events, 17.3 us)
Async XLA Ops:
  7.2 502.3 %copy-start = (bf16[1024,256]{1,0:T(8,128)(2,1)S(1)}, bf16[1024,256]{1,0:T(8,128)(2,1)}, u32[]{:S(2)}) copy-start(bf16[1024,256]{1,0:T(8,128)(2,1)} %param.5) | copy-start | bytes 1572868
  7.2 863.6 %reduce-scatter.4.cloned.1.call-start = ((), (), s32[]{:S(2)}) async-start(), calls=%async_computation.3 | async-start | bytes 10485760
  7.2 4.7 collective-permute-start
  13.0 13.2 %collective-permute-start.1 = (bf16[2,1024,128]{2,1,0:T(8,128)(2,1)S(1)}, bf16[2,1024,128]{2,1,0:T(8,128)(2,1)S(1)}, u32[]{:S(2)}, u32[]{:S(2)}) collective-permute-start(bf16[2,1024,128]{2,1,0:T(8,128)(2,1)S(1)} %pad_maximum_fusion.4), channel_id=1, source_target_pairs={{0,2},{1,3},{2,0},{3,1},{4,6},{5,7},{6,4},{7,5},{8,10},{9,11},{10,... | collective-permute-start | bytes 1572872 | tf_op jit(solution)/shard_map/ppermute | solution.py:17
  27.3 48.4 %collective-permute-start.2 = (bf16[4,1024,128]{2,1,0:T(8,128)(2,1)}, bf16[4,1024,128]{2,1,0:T(8,128)(2,1)S(1)}, u32[]{:S(2)}, u32[]{:S(2)}) collective-permute-start(bf16[4,1024,128]{2,1,0:T(8,128)(2,1)} %pad_maximum_fusion.3), channel_id=1, source_target_pairs={{0,4},{1,5},{2,6},{3,7},{4,0},{5,1},{6,2},{7,3},{8,12},{9,13},{10,... | collective-permute-start | bytes 3145736 | tf_op jit(solution)/shard_map/ppermute | solution.py:17
  75.9 1.0 copy-start.5
  75.9 1.3 copy-start.6
  77.2 95.8 %collective-permute-start.3 = (bf16[8,1024,128]{2,1,0:T(8,128)(2,1)S(1)}, bf16[8,1024,128]{2,1,0:T(8,128)(2,1)}, u32[]{:S(2)}, u32[]{:S(2)}) collective-permute-start(bf16[8,1024,128]{2,1,0:T(8,128)(2,1)S(1)} %pad_maximum_fusion.2), channel_id=1, source_target_pairs={{0,8},{1,9},{2,10},{3,11},{4,12},{5,13},{6,14},{7,15},{8,0},{9,1},... | collective-permute-start | bytes 6291464 | tf_op jit(solution)/shard_map/ppermute | solution.py:17
  175.4 2.7 copy-start.4
  178.1 90.7 %collective-permute-start.4 = (bf16[16,1024,128]{2,1,0:T(8,128)(2,1)}, bf16[16,1024,128]{2,1,0:T(8,128)(2,1)}, u32[]{:S(2)}, u32[]{:S(2)}) collective-permute-start(bf16[16,1024,128]{2,1,0:T(8,128)(2,1)} %pad_maximum_fusion.1), channel_id=1, source_target_pairs={{0,16},{1,17},{2,18},{3,19},{4,20},{5,21},{6,22},{7,23},{8,24},{9,... | collective-permute-start | bytes 12582920 | tf_op jit(solution)/shard_map/ppermute | solution.py:17
  274.3 10.1 %copy-start.7 = (s32[64,128]{1,0:T(8,128)S(1)}, s32[64,128]{1,0:T(8,128)}, u32[]{:S(2)}) copy-start(s32[64,128]{1,0:T(8,128)} %param.7) | copy-start | bytes 98308
  281.7 181.2 %collective-permute-start.5 = (bf16[32,1024,128]{2,1,0:T(8,128)(2,1)}, bf16[32,1024,128]{2,1,0:T(8,128)(2,1)}, u32[]{:S(2)}, u32[]{:S(2)}) collective-permute-start(bf16[32,1024,128]{2,1,0:T(8,128)(2,1)} %pad_maximum_fusion), channel_id=1, source_target_pairs={{0,32},{1,33},{2,34},{3,35},{4,36},{5,37},{6,38},{7,39},{8,40},{9,... | collective-permute-start | bytes 25165832 | tf_op jit(solution)/shard_map/ppermute | solution.py:17
  469.2 3.2 copy-start.2
  469.2 5.7 copy-start.3
  861.8 9.0 %copy-start.1 = (bf16[1024,256]{1,0:T(8,128)(2,1)S(1)}, bf16[1024,256]{1,0:T(8,128)(2,1)}, u32[]{:S(2)}) copy-start(bf16[1024,256]{1,0:T(8,128)(2,1)} %param.5) | copy-start | bytes 1572868
Sparse Core Ops, SparseCore 0:
  740.9 79.5 reduce-scatter.3
